TPU v7x, 32 devices: a whole 2x2x4 slice. The times are simulated.
32 devices in a mesh: groups: 2 (over x), blk: 8 (over z, y), dp: 2 (over core).
Axes of the slice: x: 2, y: 2, z: 4, core: 2. Of those that a mesh axis runs over, the one named last changes fastest.
Arguments:
- particles: bfloat16 [32768, 4096], P(('groups', 'blk', 'dp')), parts along dimension 0, may hold values from -44 to 44
- defocus: int32 [32768], P(('groups', 'blk', 'dp')), parts along dimension 0, may hold values from 0 to 15
- pick_dest: int32 [32768, 1], P(('groups', 'blk', 'dp')), parts along dimension 0, may hold values from 0 to 15; in each aligned block of 1024 rows (0 to 1023, 1024 to 2047, ...) at most 128 rows name the same one
- references: bfloat16 [192, 4096], P(('groups', 'blk')), parts along dimension 0, may hold values from -4 to 4
- ctf_table: float32 [32, 4096], P('groups'), parts along dimension 0, may hold values from 0.1 to 1
Outputs:
- weighted_sums: float32 [192, 4096], P(('groups', 'blk', 'dp')), parts along dimension 0
- ctf_weights: float32 [192, 4096], P(('groups', 'blk', 'dp')), parts along dimension 0
- posterior: float32 [65536, 96], P(('groups', 'blk', 'dp')), parts along dimension 0
There are 2 independent parts, one for each index of `groups`. A program takes and returns all parts, laid end to end along the dimension named above; each array names one. Nothing has to cross between parts.
Inputs may be any that keep to these rules, and one draw needn't show every extreme that they name: `pick_dest`: of the particles that one device holds, at most 128 name any one destination, and in every draw some device sends exactly 128 to one destination.
All inputs are finite; a program needn't handle non-finite values.
Results may differ from a plain program's by a relative error of at most 0.0028.
Values may be sent and summed in bfloat16 or wider, within the bound.
A program may use at most 128 MiB of HBM per device.

v0:
```python
import math

import jax
import jax.numpy as jnp
from jax import lax
from jax.sharding import PartitionSpec as P

PIX = 4096


def lookup(class_ids, table_rows):
    return (class_ids[:, None] == jnp.arange(table_rows, dtype=jnp.int32)[None, :]).astype(
        jnp.float32
    )


def per_device(particles, defocus, pick_dest, references, ctf_table):
    held_rows = particles.shape[0]
    table_rows = ctf_table.shape[0]
    kr_total = references.shape[0] * lax.axis_size("blk")
    device_count = lax.axis_size(("blk", "dp"))
    capacity = max(2, 2 * held_rows // device_count)
    recv_rows = device_count * capacity
    rows_mine = kr_total // device_count
    score_scale = 1.0 / math.sqrt(PIX)
    ctf_square = ctf_table * ctf_table
    own_onehot = lookup(defocus, table_rows)
    modulation = jnp.dot(own_onehot, ctf_table, precision=lax.Precision.HIGHEST)
    modulated = (particles.astype(jnp.float32) * modulation).astype(jnp.bfloat16)
    destination = pick_dest[:, 0]
    dest_hot = (destination[:, None] == jnp.arange(device_count, dtype=jnp.int32)[None, :]).astype(
        jnp.int32
    )
    earlier = jnp.cumsum(dest_hot, axis=0) - dest_hot
    ranking = jnp.sum(earlier * dest_hot, axis=1)
    slot_index = destination * capacity + ranking
    ref_piece = lax.all_gather(references, "blk", axis=0, tiled=True)
    cross_term = lax.dot_general(
        modulated, ref_piece, (((1,), (1,)), ((), ())), preferred_element_type=jnp.float32
    )
    piece_float = ref_piece.astype(jnp.float32)
    quadratic = 0.5 * lax.dot_general(
        ctf_square,
        piece_float * piece_float,
        (((1,), (1,)), ((), ())),
        precision=lax.Precision.HIGHEST,
    )
    scores = score_scale * (
        cross_term - jnp.dot(own_onehot, quadratic, precision=lax.Precision.HIGHEST)
    )
    largest = jnp.max(scores, axis=1, keepdims=True)
    exponent = jnp.exp(scores - largest)
    weights = exponent / jnp.sum(exponent, axis=1, keepdims=True)
    send_weights = jnp.zeros((recv_rows, kr_total), jnp.float32).at[slot_index].set(weights)
    posterior = lax.all_to_all(send_weights, ("blk", "dp"), split_axis=0, concat_axis=0, tiled=True)
    weights_low = weights.astype(jnp.bfloat16)
    weighted_sums = lax.psum_scatter(
        lax.dot_general(
            weights_low, modulated, (((0,), (0,)), ((), ())), preferred_element_type=jnp.float32
        ),
        ("blk", "dp"),
        scatter_dimension=0,
        tiled=True,
    )
    class_sums = lax.dot_general(
        own_onehot, weights, (((0,), (0,)), ((), ())), precision=lax.Precision.HIGHEST
    )
    totals = lax.psum(class_sums, ("blk", "dp"))
    own_sums = lax.dynamic_slice_in_dim(
        totals, lax.axis_index(("blk", "dp")) * rows_mine, rows_mine, 1
    )
    ctf_weights = lax.dot_general(
        own_sums, ctf_square, (((0,), (0,)), ((), ())), precision=lax.Precision.HIGHEST
    )
    return (weighted_sums, ctf_weights, posterior)


def solution(mesh):
    placed = (
        P(("groups", "blk", "dp"), None),
        P(("groups", "blk", "dp")),
        P(("groups", "blk", "dp"), None),
        P(("groups", "blk"), None),
        P("groups", None),
    )
    return jax.shard_map(
        per_device,
        mesh=mesh,
        in_specs=placed,
        out_specs=(
            P(("groups", "blk", "dp"), None),
            P(("groups", "blk", "dp"), None),
            P(("groups", "blk", "dp"), None),
        ),
        check_vma=False,
    )
```

profile of v0, /device:TPU:0, one launch (start us, length us, event | category | flops | bytes accessed | tf_op | source)
XLA Modules:
  0.0 189.0 jit_solution(3554859009608589075)
XLA Ops:
  0.6 34.8 %all-gather = bf16[8,12,4096]{2,1,0:T(8,128)(2,1)S(1)} all-gather(bf16[1,12,4096]{2,1,0:T(8,128)(2,1)} %bitcast.40), channel_id=1, replica_groups=mesh['groups'=2,'blk'=8,'dp'=2] {'blk'}, dimensions={0}, use_global_device_ids=true | all-gather | bytes 884736 | tf_op jit(solution)/shard_map/all_gather | solution.py:37
  35.6 2.3 %fusion.5 = f32[16,96]{1,0:T(8,128)S(1)} fusion(bf16[96,4096]{1,0:T(8,128)(2,1)S(1)} %reshape.38, f32[16,4096]{1,0:T(8,128)} %param.9), kind=kOutput, calls=%fused_computation.7 | convolution fusion | flops 76350976 | bytes 1054720 | tf_op jit(solution)/shard_map/dot_general | solution.py:42
  37.9 9.8 %multiply_convert_fusion = bf16[1024,4096]{1,0:T(8,128)(2,1)S(1)} fusion(bf16[1024,4096]{1,0:T(8,128)(2,1)} %param.5, f32[16,4096]{1,0:T(8,128)} %param.9, s32[1024]{0:T(1024)} %param.6), kind=kOutput, calls=%fused_computation.1 | convolution fusion | flops 817905664 | bytes 17043456 | tf_op jit(solution)/shard_map/dot_general | solution.py:28
  47.7 3.2 %copy-done = bf16[1024,4096]{1,0:T(8,128)(2,1)} copy-done((bf16[1024,4096]{1,0:T(8,128)(2,1)}, bf16[1024,4096]{1,0:T(8,128)(2,1)S(1)}, u32[]{:S(2)}) %copy-start) | copy-done | bytes 8388632
  50.9 2.7 %fusion.28 = f32[1024,96]{0,1:T(8,128)S(1)} fusion(bf16[1024,4096]{1,0:T(8,128)(2,1)S(1)} %multiply_convert_fusion, bf16[96,4096]{1,0:T(8,128)(2,1)S(1)} %reshape.38), kind=kOutput, calls=%fused_computation.37 | convolution fusion | flops 805306368 | bytes 9568256 | tf_op jit(solution)/shard_map/dot_general | solution.py:38
  53.6 0.6 fusion.27
  54.4 0.2 copy.20
  54.6 4.5 %reduce-window.6 = s32[16,8,128]{2,1,0:T(8,128)S(1)} reduce-window(s32[16,8,128]{2,1,0:T(8,128)S(1)} %fusion.24, s32[]{:T(128)} %constant.6.clone.1), window={size=1x1x128 pad=0_0x0_0x127_0}, to_apply=%region_4.5 | reduce-window | flops 2080768 | bytes 131076 | tf_op jit(solution)/shard_map/reduce-window
  59.6 3.3 %scatter_custom_fusion = f32[2048,96]{1,0:T(8,128)S(1)} fusion(s32[1024]{0:T(1024)S(1)} %bitcast.45, f32[1024,96]{1,0:T(8,128)S(1)} %copy.20, f32[]{:T(128)} %constant.15.clone.1), kind=kCustom, calls=%fused_computation.9 | custom fusion | bytes 786436 | tf_op jit(solution)/shard_map/scatter | solution.py:54
  62.9 1.2 copy.21
  64.2 5.6 %all-to-all-start = ((f32[16,128,96]{1,2,0:T(8,128)}), f32[16,128,96]{1,2,0:T(8,128)S(1)}, u32[]{:S(2)}, u32[]{:S(2)}) async-start(f32[16,128,96]{1,2,0:T(8,128)} %copy.21), calls=%async_computation | async-start | bytes 1572864 | tf_op jit(solution)/shard_map/all_to_all | solution.py:55
  69.8 4.9 %fusion.19 = f32[96,4096]{1,0:T(8,128)S(1)} fusion(bf16[1024,4096]{1,0:T(8,128)(2,1)} %copy-done, f32[1024,96]{0,1:T(8,128)S(1)} %fusion.11), kind=kOutput, calls=%fused_computation.22 | convolution fusion | flops 805404672 | bytes 10354688 | tf_op jit(solution)/shard_map/dot_general | solution.py:58
  74.6 43.0 %fusion = f32[8,4096]{1,0:T(8,128)S(1)} fusion(f32[96,4096]{1,0:T(8,128)S(1)} %fusion.19), kind=kCustom, calls=%all-reduce-scatter | all-reduce-scatter fusion | flops 524289 | bytes 1704448
  117.7 1.3 collective-permute-start
  119.0 1.3 collective-permute-start.1
  120.3 2.2 %collective-permute-start.2 = (f32[8,4096]{1,0:T(8,128)S(1)}, f32[8,4096]{1,0:T(8,128)S(1)}, u32[]{:S(2)}, u32[]{:S(2)}) collective-permute-start(f32[8,4096]{1,0:T(8,128)S(1)} %fusion), channel_id=1, source_target_pairs={{0,3},{1,4},{2,5},{3,6},{4,7},{5,8},{6,9},{7,10},{8,11},{9,12},{10... | collective-permute-start | bytes 393224
  122.5 3.7 %collective-permute-start.3 = (f32[6,4096]{1,0:T(8,128)S(1)}, f32[6,4096]{1,0:T(8,128)S(1)}, u32[]{:S(2)}, u32[]{:S(2)}) collective-permute-start(f32[6,4096]{1,0:T(8,128)S(1)} %slice.10), channel_id=1, source_target_pairs={{0,4},{1,5},{2,6},{3,7},{4,8},{5,9},{6,10},{7,11},{8,12},{9,13},{1... | collective-permute-start | bytes 294920
  126.2 0.5 fusion.10
  126.7 57.7 %psum.7 = f32[16,96]{0,1:T(8,128)S(1)} all-reduce(f32[16,96]{0,1:T(8,128)S(1)} %fusion.10), channel_id=1, replica_groups=mesh['groups'=2,'blk'=8,'dp'=2] {'blk','dp'}, use_global_device_ids=true, to_apply=%region_3.4 | all-reduce | flops 1536 | bytes 12288 | tf_op jit(solution)/shard_map/psum | solution.py:68
  184.4 0.9 fusion.16
  185.3 0.6 dynamic-slice.4
  186.6 0.8 concatenate
  187.4 0.7 constant_dynamic-slice_fusion
  188.1 0.9 copy_bitcast_fusion
  (27 shorter events, 0.8 us)
Async XLA Ops:
  47.7 3.2 %copy-start = (bf16[1024,4096]{1,0:T(8,128)(2,1)}, bf16[1024,4096]{1,0:T(8,128)(2,1)S(1)}, u32[]{:S(2)}) copy-start(bf16[1024,4096]{1,0:T(8,128)(2,1)S(1)} %multiply_convert_fusion) | copy-start | bytes 25165828
  50.9 2.7 %copy-start.2 = (s32[1024]{0:T(1024)S(1)}, s32[1024]{0:T(1024)}, u32[]{:S(2)}) copy-start(s32[1024]{0:T(1024)} %param.6) | copy-start | bytes 12292
  50.9 3.7 %copy-start.3 = (s32[1024,1]{0,1:T(1,128)S(1)}, s32[1024,1]{0,1:T(1,128)}, u32[]{:S(2)}) copy-start(s32[1024,1]{0,1:T(1,128)} %param.7) | copy-start | bytes 12292
  64.2 123.9 %all-to-all-start = ((f32[16,128,96]{1,2,0:T(8,128)}), f32[16,128,96]{1,2,0:T(8,128)S(1)}, u32[]{:S(2)}, u32[]{:S(2)}) async-start(f32[16,128,96]{1,2,0:T(8,128)} %copy.21), calls=%async_computation | async-start | bytes 1572864 | tf_op jit(solution)/shard_map/all_to_all | solution.py:55
  69.7 114.7 %copy-start.1 = (f32[16,4096]{1,0:T(8,128)S(1)}, f32[16,4096]{1,0:T(8,128)}, u32[]{:S(2)}) copy-start(f32[16,4096]{1,0:T(8,128)} %param.9) | copy-start | bytes 786436
  69.8 115.6 %copy-start.4 = (u32[32]{0:T(128)S(1)}, u32[32]{0:T(128)}, u32[]{:S(2)}) copy-start(u32[32]{0:T(128)} %constant.37) | copy-start | bytes 388
  117.7 68.9 %collective-permute-start = (f32[8,4096]{1,0:T(8,128)S(1)}, f32[8,4096]{1,0:T(8,128)S(1)}, u32[]{:S(2)}, u32[]{:S(2)}) collective-permute-start(f32[8,4096]{1,0:T(8,128)S(1)} %fusion), channel_id=1, source_target_pairs={{0,1},{1,2},{2,3},{3,4},{4,5},{5,6},{6,7},{7,8},{8,9},{9,10},{10,1... | collective-permute-start | bytes 393224
  119.0 67.6 %collective-permute-start.1 = (f32[8,4096]{1,0:T(8,128)S(1)}, f32[8,4096]{1,0:T(8,128)S(1)}, u32[]{:S(2)}, u32[]{:S(2)}) collective-permute-start(f32[8,4096]{1,0:T(8,128)S(1)} %fusion), channel_id=1, source_target_pairs={{0,2},{1,3},{2,4},{3,5},{4,6},{5,7},{6,8},{7,9},{8,10},{9,11},{10,... | collective-permute-start | bytes 393224
  120.3 66.3 %collective-permute-start.2 = (f32[8,4096]{1,0:T(8,128)S(1)}, f32[8,4096]{1,0:T(8,128)S(1)}, u32[]{:S(2)}, u32[]{:S(2)}) collective-permute-start(f32[8,4096]{1,0:T(8,128)S(1)} %fusion), channel_id=1, source_target_pairs={{0,3},{1,4},{2,5},{3,6},{4,7},{5,8},{6,9},{7,10},{8,11},{9,12},{10... | collective-permute-start | bytes 393224
  122.5 64.0 %collective-permute-start.3 = (f32[6,4096]{1,0:T(8,128)S(1)}, f32[6,4096]{1,0:T(8,128)S(1)}, u32[]{:S(2)}, u32[]{:S(2)}) collective-permute-start(f32[6,4096]{1,0:T(8,128)S(1)} %slice.10), channel_id=1, source_target_pairs={{0,4},{1,5},{2,6},{3,7},{4,8},{5,9},{6,10},{7,11},{8,12},{9,13},{1... | collective-permute-start | bytes 294920
where the time goes:
time: 189 us
  blocking collectives  136 us (72%)
  matrix products  21.6 us (11%)
  starting transfers between devices  14.1 us (7%)
  local copies, waits for them, and re-layouts  11.5 us (6%)
  other arithmetic  4.82 us (3%)
    psum x1, blocking collectives, per_device(): totals = lax.psum(class_sums, ('blk', 'dp'))  57.7 us
    unnamed x1, blocking collectives  43 us
    all_gather x1, blocking collectives, per_device(): ref_piece = lax.all_gather(references, 'blk', axis=0, tiled=True)  34.8 us
    dot_general x1, matrix products, per_device(): modulation = jnp.dot(own_onehot, ctf_table, precision=lax.Precision.HIGHEST)  9.82 us
    unnamed x4, starting transfers between devices  8.47 us
    all_to_all x1, starting transfers between devices, per_device(): lax.all_to_all(send_weights, ('blk', 'dp'), split_axis=0, concat_axis=0,...  5.59 us
    unnamed x15, local copies, waits for them, and re-layouts  5.48 us
    dot_general x1, matrix products, per_device(): lax.dot_general(weights_low, modulated, (((0,), (0,)), ((), ())), preferr...  4.87 us
  transfers between devices with their start and end apart: 5, of which 0 were waited for; matrix products, arithmetic and copies ran while one was open for 27% of the time, Pallas kernels for 0%

commit v1 on v0

v1 whole, which is shorter than its diff:
```python
import functools
import math

import jax
import jax.numpy as jnp
from jax import lax
from jax.experimental import pallas as pl
from jax.experimental.pallas import tpu as pltpu
from jax.sharding import PartitionSpec as P

MESH = pl.DeviceIdType.MESH
BF = jnp.bfloat16
F32 = jnp.float32
PAD = 16
LANES = 128
ROWS = 128
COLS = 512
SCORE_ROWS = 256


def dot_nt(left, right, **kw):
    return lax.dot_general(
        left, right, (((1,), (1,)), ((), ())), preferred_element_type=F32, **kw
    )


def dot_nn(left, right, **kw):
    return lax.dot_general(
        left, right, (((1,), (0,)), ((), ())), preferred_element_type=F32, **kw
    )


def split3(value):
    high = value.astype(BF)
    rest = value - high.astype(F32)
    middle = rest.astype(BF)
    low = (rest - middle.astype(F32)).astype(BF)
    return high, middle, low


def kernel(
    n_blk, n_dp, own_rows, capacity,
    particles, defocus, dest, refs_in, ctf_in,
    sums_out, ctf_out, post_out,
    part, refs, table, square, onehot_t, onehot, slots, weights, low,
    kept, mate_send, mate_recv, chip_send, chip_recv, class_send, class_recv,
    final_send, final_recv, cfinal_send, cfinal_recv, post_send, post_recv,
    part_sem, ref_ssem, ref_rsem, fwd_ssem, fwd_rsem, post_ssem, post_rsem,
    mate_ssem, mate_rsem, chip_ssem, chip_rsem, class_ssem, class_rsem,
    final_ssem, final_rsem,
):
    held, pix = part.shape
    mod = part
    half = pix // n_dp
    devices = n_blk * n_dp
    padded = n_blk * PAD
    kinds = ctf_in.shape[0]
    rows_mine = own_rows // n_dp
    score_scale = 1.0 / math.sqrt(pix)
    blk = lax.axis_index("blk")
    core = lax.axis_index("dp")
    me = blk * n_dp + core
    mate = {"dp": 1 - core}
    my_cols = pl.ds(pl.multiple_of(core * half, half), half)
    mate_cols = pl.ds(pl.multiple_of((1 - core) * half, half), half)

    loads = []
    for chunk in range(held // ROWS):
        copy = pltpu.make_async_copy(
            particles.at[pl.ds(chunk * ROWS, ROWS)],
            part.at[pl.ds(chunk * ROWS, ROWS)],
            part_sem.at[chunk],
        )
        copy.start()
        loads.append(copy)

    barrier = pltpu.get_barrier_semaphore()
    for step in range(1, devices):
        other = lax.rem(me + step, devices)
        pl.semaphore_signal(
            barrier, inc=1, device_id={"blk": other // n_dp, "dp": lax.rem(other, n_dp)},
            device_id_type=MESH,
        )
    refs[blk, 0:own_rows, :] = refs_in[...]
    zeros = jnp.zeros((PAD - own_rows, pix), BF)
    refs[blk, own_rows:PAD, :] = zeros
    pl.semaphore_wait(barrier, devices - 1)

    ref_copies = []
    for step in range(1, n_blk):
        target = lax.rem(blk + step, n_blk)
        piece = refs.at[blk, :, my_cols]
        copy = pltpu.make_async_remote_copy(
            src_ref=piece, dst_ref=piece,
            send_sem=ref_ssem.at[step], recv_sem=ref_rsem.at[step],
            device_id={"blk": target}, device_id_type=MESH,
        )
        copy.start()
        ref_copies.append(copy)

    kind_rows = lax.broadcasted_iota(jnp.int32, (LANES, held), 0)
    class_row = defocus[...]
    hot = jnp.where(
        (lax.rem(kind_rows, kinds) == class_row) & (kind_rows < 3 * kinds), 1.0, 0.0
    ).astype(F32)
    onehot_t[...] = hot
    onehot[...] = hot.T.astype(BF)
    table[...] = jnp.zeros_like(table)
    square[...] = jnp.zeros_like(square)
    ctf = ctf_in[...]
    for index, value in enumerate(split3(ctf)):
        table[index * kinds:(index + 1) * kinds, :] = value
    for index, value in enumerate(split3(ctf * ctf)):
        square[index * kinds:(index + 1) * kinds, :] = value

    forwards = []

    def forward(step):
        ref_copies[step - 1].wait_recv()
        source = lax.rem(blk + n_blk - step, n_blk)
        piece = refs.at[source, :, my_cols]
        copy = pltpu.make_async_remote_copy(
            src_ref=piece, dst_ref=piece,
            send_sem=fwd_ssem.at[step], recv_sem=fwd_rsem.at[step],
            device_id=mate, device_id_type=MESH,
        )
        copy.start()
        forwards.append(copy)

    pending = list(range(1, n_blk))
    per_chunk = -(-(n_blk - 1) // (held // ROWS))
    for chunk in range(held // ROWS):
        loads[chunk].wait()
        base = chunk * ROWS
        chosen = onehot[base:base + ROWS, :]

        def modulate(block, carry):
            columns = pl.ds(pl.multiple_of(block * COLS, COLS), COLS)
            factor = dot_nn(chosen, table[:, columns])
            mod[base:base + ROWS, columns] = (
                part[base:base + ROWS, columns].astype(F32) * factor
            ).astype(BF)
            return carry

        lax.fori_loop(0, pix // COLS, modulate, 0)
        for _ in range(per_chunk):
            if pending and chunk > 0 or len(pending) > held // ROWS:
                forward(pending.pop(0))
    while pending:
        forward(pending.pop(0))

    dest_row = dest[...]
    dest_hot = jnp.where(
        lax.broadcasted_iota(jnp.int32, (devices, held), 0) == dest_row, 1.0, 0.0
    ).astype(F32)
    before = jnp.where(
        lax.broadcasted_iota(jnp.int32, (held, held), 0)
        < lax.broadcasted_iota(jnp.int32, (held, held), 1), 1.0, 0.0
    ).astype(BF)
    earlier = dot_nn(dest_hot.astype(BF), before)
    rank = jnp.sum(earlier * dest_hot, axis=0, keepdims=True)
    slots[...] = dest_row.astype(F32) * float(capacity) + rank

    for copy in forwards:
        copy.wait_recv()

    def gather_square(block, total):
        columns = pl.ds(pl.multiple_of(block * COLS, COLS), COLS)
        value = refs[:, :, columns].reshape(padded, COLS).astype(F32)
        value = value * value
        high = value.astype(BF)
        rest = (value - high.astype(F32)).astype(BF)
        factor = square[:, columns]
        return total + dot_nt(high, factor) + dot_nt(rest, factor)

    quadratic = 0.5 * lax.fori_loop(
        0, pix // COLS, gather_square, jnp.zeros((padded, LANES), F32)
    )
    valid = lax.rem(lax.broadcasted_iota(jnp.int32, (padded, SCORE_ROWS), 0), PAD) < own_rows
    every_ref = refs[...].reshape(padded, pix)
    for chunk in range(held // SCORE_ROWS):
        span = slice(chunk * SCORE_ROWS, (chunk + 1) * SCORE_ROWS)
        cross = dot_nt(every_ref, mod[span, :])
        offset = dot_nn(quadratic, onehot_t[:, span], precision=lax.Precision.HIGHEST)
        scores = jnp.where(valid, (cross - offset) * score_scale, -1e30)
        largest = jnp.max(scores, axis=0, keepdims=True)
        exponent = jnp.exp(scores - largest)
        share = exponent * (1.0 / jnp.sum(exponent, axis=0, keepdims=True))
        weights[:, span] = share
        low[:, span] = share.astype(BF)

    mate_copies = []
    for block in range(half // COLS):
        source = pl.ds(pl.multiple_of((1 - core) * half + block * COLS, COLS), COLS)
        local = pl.ds(block * COLS, COLS)
        mate_send[:, :, local] = dot_nn(low[...], mod[:, source]).reshape(
            n_blk, PAD, COLS).astype(BF)
        copy = pltpu.make_async_remote_copy(
            src_ref=mate_send.at[:, :, local], dst_ref=mate_recv.at[:, :, local],
            send_sem=mate_ssem.at[block], recv_sem=mate_rsem.at[block],
            device_id=mate, device_id_type=MESH,
        )
        copy.start()
        mate_copies.append(copy)
    for block in range(half // COLS):
        source = pl.ds(pl.multiple_of(core * half + block * COLS, COLS), COLS)
        local = pl.ds(block * COLS, COLS)
        kept[:, :, local] = dot_nn(low[...], mod[:, source]).reshape(n_blk, PAD, COLS)
    class_send[...] = dot_nt(
        weights[...], onehot_t[...], precision=lax.Precision.HIGHEST
    ).reshape(n_blk, PAD, LANES)
    chip_copies = []
    for step in range(1, n_blk):
        target = lax.rem(blk + step, n_blk)
        copy = pltpu.make_async_remote_copy(
            src_ref=class_send.at[target], dst_ref=class_recv.at[step],
            send_sem=class_ssem.at[step], recv_sem=class_rsem.at[step],
            device_id={"blk": target}, device_id_type=MESH,
        )
        copy.start()
        chip_copies.append(copy)
    for block, copy in enumerate(mate_copies):
        copy.wait_recv()
        local = pl.ds(block * COLS, COLS)
        both = kept[:, :, local] + mate_recv[:, :, local].astype(F32)
        kept[:, :, local] = both
        chip_send[:, :, local] = both.astype(BF)
    for step in range(1, n_blk):
        target = lax.rem(blk + step, n_blk)
        copy = pltpu.make_async_remote_copy(
            src_ref=chip_send.at[target],
            dst_ref=chip_recv.at[step],
            send_sem=chip_ssem.at[step], recv_sem=chip_rsem.at[step],
            device_id={"blk": target}, device_id_type=MESH,
        )
        copy.start()
        chip_copies.append(copy)

    kept_refs = n_blk * own_rows
    pick_row = lax.broadcasted_iota(jnp.int32, (kept_refs, padded), 0)
    pick = jnp.where(
        (pick_row // own_rows) * PAD + lax.rem(pick_row, own_rows)
        == lax.broadcasted_iota(jnp.int32, (kept_refs, padded), 1), 1.0, 0.0
    ).astype(BF)
    compact = dot_nn(pick, low[...]).astype(BF)
    slot_row = slots[...]
    place = lax.broadcasted_iota(jnp.int32, (capacity, held), 0)
    post_copies = []
    for step in list(range(1, devices)) + [0]:
        other = lax.rem(me + step, devices)
        chosen = jnp.where(
            (place + other * capacity).astype(F32) == slot_row, 1.0, 0.0
        ).astype(BF)
        block = dot_nt(compact, chosen)
        if step == 0:
            post_recv[0] = block.astype(BF)
        else:
            post_send[step] = block.astype(BF)
            copy = pltpu.make_async_remote_copy(
                src_ref=post_send.at[step], dst_ref=post_recv.at[step],
                send_sem=post_ssem.at[step], recv_sem=post_rsem.at[step],
                device_id={"blk": other // n_dp, "dp": lax.rem(other, n_dp)},
                device_id_type=MESH,
            )
            copy.start()
            post_copies.append(copy)

    total = kept[blk]
    classes = class_send[blk]
    for copy in chip_copies:
        copy.wait_recv()
    for step in range(1, n_blk):
        total = total + chip_recv[step].astype(F32)
        classes = classes + class_recv[step]
    first, second = total[0:rows_mine], total[rows_mine:own_rows]
    final_send[0:rows_mine, :] = jnp.where(core == 0, second, first)
    cfinal_send[...] = classes
    finals = []
    for source, target, index in ((final_send, final_recv, 0), (cfinal_send, cfinal_recv, 1)):
        copy = pltpu.make_async_remote_copy(
            src_ref=source, dst_ref=target,
            send_sem=final_ssem.at[index], recv_sem=final_rsem.at[index],
            device_id=mate, device_id_type=MESH,
        )
        copy.start()
        finals.append(copy)
    sums_out[:, my_cols] = jnp.where(core == 0, first, second)

    for step in [0] + list(range(1, devices)):
        if step:
            post_copies[step - 1].wait_recv()
    for source in range(devices):
        step = lax.rem(me + devices - source, devices)
        post_out[:, source * capacity:(source + 1) * capacity] = post_recv[step].astype(F32)

    for copy in finals:
        copy.wait_recv()
    sums_out[:, mate_cols] = final_recv[0:rows_mine, :]
    classes = classes + cfinal_recv[...]
    mine = jnp.where(core == 0, classes[0:rows_mine], classes[rows_mine:own_rows])
    mine = mine[:, 0:kinds]

    ctf_out[...] = dot_nn(
        mine, ctf_in[...] * ctf_in[...], precision=lax.Precision.HIGHEST
    )

    for copy in ref_copies + forwards + mate_copies + chip_copies + post_copies + finals:
        copy.wait_send()


def per_device(particles, defocus, pick_dest, references, ctf_table):
    held, pix = particles.shape
    own_rows = references.shape[0]
    n_blk, n_dp = lax.axis_size("blk"), lax.axis_size("dp")
    devices = n_blk * n_dp
    capacity = max(2, 2 * held // devices)
    kept_refs = n_blk * own_rows
    padded = n_blk * PAD
    half = pix // n_dp
    rows_mine = own_rows // n_dp
    vmem = pl.BlockSpec(memory_space=pltpu.VMEM)
    dma = pltpu.SemaphoreType.DMA
    sums, weights, posterior = pl.pallas_call(
        functools.partial(kernel, n_blk, n_dp, own_rows, capacity),
        out_shape=(
            jax.ShapeDtypeStruct((rows_mine, pix), F32),
            jax.ShapeDtypeStruct((rows_mine, pix), F32),
            jax.ShapeDtypeStruct((kept_refs, devices * capacity), F32),
        ),
        in_specs=[pl.BlockSpec(memory_space=pl.ANY), vmem, vmem, vmem, vmem],
        out_specs=(vmem, vmem, vmem),
        scratch_shapes=[
            pltpu.VMEM((held, pix), BF),
            pltpu.VMEM((n_blk, PAD, pix), BF),
            pltpu.VMEM((LANES, pix), BF),
            pltpu.VMEM((LANES, pix), BF),
            pltpu.VMEM((LANES, held), F32),
            pltpu.VMEM((held, LANES), BF),
            pltpu.VMEM((1, held), F32),
            pltpu.VMEM((padded, held), F32),
            pltpu.VMEM((padded, held), BF),
            pltpu.VMEM((n_blk, PAD, half), F32),
            pltpu.VMEM((n_blk, PAD, half), BF),
            pltpu.VMEM((n_blk, PAD, half), BF),
            pltpu.VMEM((n_blk, PAD, half), BF),
            pltpu.VMEM((n_blk, PAD, half), BF),
            pltpu.VMEM((n_blk, PAD, LANES), F32),
            pltpu.VMEM((n_blk, PAD, LANES), F32),
            pltpu.VMEM((8, half), F32),
            pltpu.VMEM((8, half), F32),
            pltpu.VMEM((PAD, LANES), F32),
            pltpu.VMEM((PAD, LANES), F32),
            pltpu.VMEM((devices, kept_refs, capacity), BF),
            pltpu.VMEM((devices, kept_refs, capacity), BF),
            dma((held // ROWS,)),
            dma((n_blk,)), dma((n_blk,)), dma((n_blk,)), dma((n_blk,)),
            dma((devices,)), dma((devices,)),
            dma((half // COLS,)), dma((half // COLS,)),
            dma((n_blk,)), dma((n_blk,)), dma((n_blk,)), dma((n_blk,)),
            dma((2,)), dma((2,)),
        ],
        compiler_params=pltpu.CompilerParams(
            collective_id=0, has_side_effects=True, vmem_limit_bytes=60 << 20
        ),
        name="em_step",
    )(
        particles,
        defocus.reshape(1, held),
        pick_dest.reshape(1, held),
        references,
        ctf_table,
    )
    return sums, weights, posterior.T


def solution(mesh):
    placed = (
        P(("groups", "blk", "dp"), None),
        P(("groups", "blk", "dp")),
        P(("groups", "blk", "dp"), None),
        P(("groups", "blk"), None),
        P("groups", None),
    )
    return jax.shard_map(
        per_device,
        mesh=mesh,
        in_specs=placed,
        out_specs=(
            P(("groups", "blk", "dp"), None),
            P(("groups", "blk", "dp"), None),
            P(("groups", "blk", "dp"), None),
        ),
        check_vma=False,
    )
```

time: 189 us -> 58.6 us (0.31)
  the two profiles are of different devices: /device:TPU:0 before, /device:TPU:13 now
where the time goes in v1:
time: 58.6 us; the launch traced here: 58.4 us
  Pallas kernels  52.6 us (90%)
  local copies, waits for them, and re-layouts  5.2 us (9%)
  between operations  0.64 us (1%)
    pallas_call x1, Pallas kernels, per_device(): pl.pallas_call(functools.partial(kernel, n_blk, n_dp, own_rows, capacity)...  52.6 us
    unnamed x3, local copies, waits for them, and re-layouts  5.2 us

profile of v1, /device:TPU:13, one launch (start us, length us, event | category | flops | bytes accessed | tf_op | source)
XLA Modules:
  0.0 58.4 jit_solution(9803231214421967655)
XLA Ops:
  0.6 52.6 %em_step.1 = (f32[6,4096]{1,0:T(8,128)}, f32[6,4096]{1,0:T(8,128)}, f32[96,2048]{1,0:T(8,128)}) custom-call(bf16[1024,4096]{1,0:T(8,128)(2,1)} %particles.1, s32[1,1024]{1,0:T(1,128)} %bitcast.4, s32[1,1024]{1,0:T(1,128)} %bitcast.5, bf16[12,4096]{1,0:T(8,128)(2,1)} %refs_in.1, f32[16,4096]{1,0:T(8,128)} %ctf_in.1), custom_call_target="tpu_custom_call" | custom-call | tf_op jit(solution)/shard_map/em_step/pallas_call | solution.py:323
  53.2 1.6 %copy.11 = f32[6,4096]{1,0:T(8,128)} copy(f32[6,4096]{1,0:T(8,128)} %get-tuple-element.12) | data formatting | bytes 196608
  54.8 1.6 %copy.12 = f32[6,4096]{1,0:T(8,128)} copy(f32[6,4096]{1,0:T(8,128)} %get-tuple-element.13) | data formatting | bytes 196608
  56.4 2.1 %copy.13 = f32[2048,96]{0,1:T(8,128)} copy(f32[2048,96]{0,1:T(8,128)} %bitcast.3) | data formatting | bytes 1572864

commit v2 on v1

--- a/solution.py
+++ b/solution.py
@@ -13,7 +13,8 @@
 F32 = jnp.float32
 PAD = 16
 LANES = 128
-ROWS = 128
+ROWS = 256
+TILE = 256
 COLS = 512
 SCORE_ROWS = 256
 
@@ -41,12 +42,12 @@
 def kernel(
     n_blk, n_dp, own_rows, capacity,
     particles, defocus, dest, refs_in, ctf_in,
-    sums_out, ctf_out, post_out,
+    sums_out, class_out, post_recv,
     part, refs, table, square, onehot_t, onehot, slots, weights, low,
-    kept, mate_send, mate_recv, chip_send, chip_recv, class_send, class_recv,
-    final_send, final_recv, cfinal_send, cfinal_recv, post_send, post_recv,
-    part_sem, ref_ssem, ref_rsem, fwd_ssem, fwd_rsem, post_ssem, post_rsem,
-    mate_ssem, mate_rsem, chip_ssem, chip_rsem, class_ssem, class_rsem,
+    kept, mate_send, mate_recv, side_send, side_recv, chip_send, chip_recv, class_send, class_recv,
+    final_send, final_recv, cfinal_send, cfinal_recv, post_send,
+    part_sem, ref_ssem, ref_rsem, near_ssem, near_rsem, fwd_ssem, fwd_rsem, post_ssem, post_rsem,
+    mate_ssem, mate_rsem, side_ssem, side_rsem, chip_ssem, chip_rsem, class_ssem, class_rsem,
     final_ssem, final_rsem,
 ):
     held, pix = part.shape
@@ -58,6 +59,10 @@
     rows_mine = own_rows // n_dp
     score_scale = 1.0 / math.sqrt(pix)
     blk = lax.axis_index("blk")
+    near = 2
+    deep = n_blk // near
+    z, y = blk // near, lax.rem(blk, near)
+    partner = {"blk": z * near + 1 - y}
     core = lax.axis_index("dp")
     me = blk * n_dp + core
     mate = {"dp": 1 - core}
@@ -84,20 +89,6 @@
     refs[blk, 0:own_rows, :] = refs_in[...]
     zeros = jnp.zeros((PAD - own_rows, pix), BF)
     refs[blk, own_rows:PAD, :] = zeros
-    pl.semaphore_wait(barrier, devices - 1)
-
-    ref_copies = []
-    for step in range(1, n_blk):
-        target = lax.rem(blk + step, n_blk)
-        piece = refs.at[blk, :, my_cols]
-        copy = pltpu.make_async_remote_copy(
-            src_ref=piece, dst_ref=piece,
-            send_sem=ref_ssem.at[step], recv_sem=ref_rsem.at[step],
-            device_id={"blk": target}, device_id_type=MESH,
-        )
-        copy.start()
-        ref_copies.append(copy)
-
     kind_rows = lax.broadcasted_iota(jnp.int32, (LANES, held), 0)
     class_row = defocus[...]
     hot = jnp.where(
@@ -113,41 +104,58 @@
     for index, value in enumerate(split3(ctf * ctf)):
         square[index * kinds:(index + 1) * kinds, :] = value
 
+    pl.semaphore_wait(barrier, devices - 1)
+
+    def send_ref(owner, send_sem, recv_sem, target):
+        piece = refs.at[owner, :, my_cols]
+        copy = pltpu.make_async_remote_copy(
+            src_ref=piece, dst_ref=piece, send_sem=send_sem, recv_sem=recv_sem,
+            device_id=target, device_id_type=MESH,
+        )
+        copy.start()
+        return copy
+
+    near_copies = [None] * deep
+    far_copies = [None] * deep
     forwards = []
-
-    def forward(step):
-        ref_copies[step - 1].wait_recv()
-        source = lax.rem(blk + n_blk - step, n_blk)
-        piece = refs.at[source, :, my_cols]
-        copy = pltpu.make_async_remote_copy(
-            src_ref=piece, dst_ref=piece,
-            send_sem=fwd_ssem.at[step], recv_sem=fwd_rsem.at[step],
-            device_id=mate, device_id_type=MESH,
-        )
-        copy.start()
-        forwards.append(copy)
-
-    pending = list(range(1, n_blk))
-    per_chunk = -(-(n_blk - 1) // (held // ROWS))
+    for step in range(1, deep):
+        far_copies[step] = send_ref(
+            blk, ref_ssem.at[step], ref_rsem.at[step],
+            {"blk": lax.rem(z + step, deep) * near + y},
+        )
+    near_copies[0] = send_ref(blk, near_ssem.at[0], near_rsem.at[0], partner)
+
+    def forward_far(step):
+        far_copies[step].wait_recv()
+        owner = lax.rem(z + deep - step, deep) * near + y
+        near_copies[step] = send_ref(owner, near_ssem.at[step], near_rsem.at[step], partner)
+        forwards.append(send_ref(owner, fwd_ssem.at[step], fwd_rsem.at[step], mate))
+
+    def forward_near(step):
+        near_copies[step].wait_recv()
+        owner = lax.rem(z + deep - step, deep) * near + 1 - y
+        index = deep + step
+        forwards.append(send_ref(owner, fwd_ssem.at[index], fwd_rsem.at[index], mate))
+
+    order = sorted(range(1, deep), key=lambda step: min(step, deep - step))
+    pending = [functools.partial(forward_far, step) for step in order]
+    pending += [functools.partial(forward_near, step) for step in [0] + order]
     for chunk in range(held // ROWS):
         loads[chunk].wait()
         base = chunk * ROWS
         chosen = onehot[base:base + ROWS, :]
 
-        def modulate(block, carry):
-            columns = pl.ds(pl.multiple_of(block * COLS, COLS), COLS)
+        for block in range(pix // TILE):
+            columns = slice(block * TILE, (block + 1) * TILE)
             factor = dot_nn(chosen, table[:, columns])
             mod[base:base + ROWS, columns] = (
                 part[base:base + ROWS, columns].astype(F32) * factor
             ).astype(BF)
-            return carry
-
-        lax.fori_loop(0, pix // COLS, modulate, 0)
-        for _ in range(per_chunk):
-            if pending and chunk > 0 or len(pending) > held // ROWS:
-                forward(pending.pop(0))
+        if chunk < deep - 1:
+            pending.pop(0)()
+
     while pending:
-        forward(pending.pop(0))
+        pending.pop(0)()
 
     dest_row = dest[...]
     dest_hot = jnp.where(
@@ -174,7 +182,7 @@
         return total + dot_nt(high, factor) + dot_nt(rest, factor)
 
     quadratic = 0.5 * lax.fori_loop(
-        0, pix // COLS, gather_square, jnp.zeros((padded, LANES), F32)
+        0, pix // COLS, gather_square, jnp.zeros((padded, LANES), F32), unroll=True
     )
     valid = lax.rem(lax.broadcasted_iota(jnp.int32, (padded, SCORE_ROWS), 0), PAD) < own_rows
     every_ref = refs[...].reshape(padded, pix)
@@ -202,40 +210,6 @@
         )
         copy.start()
         mate_copies.append(copy)
-    for block in range(half // COLS):
-        source = pl.ds(pl.multiple_of(core * half + block * COLS, COLS), COLS)
-        local = pl.ds(block * COLS, COLS)
-        kept[:, :, local] = dot_nn(low[...], mod[:, source]).reshape(n_blk, PAD, COLS)
-    class_send[...] = dot_nt(
-        weights[...], onehot_t[...], precision=lax.Precision.HIGHEST
-    ).reshape(n_blk, PAD, LANES)
-    chip_copies = []
-    for step in range(1, n_blk):
-        target = lax.rem(blk + step, n_blk)
-        copy = pltpu.make_async_remote_copy(
-            src_ref=class_send.at[target], dst_ref=class_recv.at[step],
-            send_sem=class_ssem.at[step], recv_sem=class_rsem.at[step],
-            device_id={"blk": target}, device_id_type=MESH,
-        )
-        copy.start()
-        chip_copies.append(copy)
-    for block, copy in enumerate(mate_copies):
-        copy.wait_recv()
-        local = pl.ds(block * COLS, COLS)
-        both = kept[:, :, local] + mate_recv[:, :, local].astype(F32)
-        kept[:, :, local] = both
-        chip_send[:, :, local] = both.astype(BF)
-    for step in range(1, n_blk):
-        target = lax.rem(blk + step, n_blk)
-        copy = pltpu.make_async_remote_copy(
-            src_ref=chip_send.at[target],
-            dst_ref=chip_recv.at[step],
-            send_sem=chip_ssem.at[step], recv_sem=chip_rsem.at[step],
-            device_id={"blk": target}, device_id_type=MESH,
-        )
-        copy.start()
-        chip_copies.append(copy)
-
     kept_refs = n_blk * own_rows
     pick_row = lax.broadcasted_iota(jnp.int32, (kept_refs, padded), 0)
     pick = jnp.where(
@@ -252,12 +226,15 @@
             (place + other * capacity).astype(F32) == slot_row, 1.0, 0.0
         ).astype(BF)
         block = dot_nt(compact, chosen)
+        post_send[step] = block.astype(BF)
         if step == 0:
-            post_recv[0] = block.astype(BF)
+            own_copy = pltpu.make_async_copy(
+                post_send.at[0], post_recv.at[me], post_rsem.at[0]
+            )
+            own_copy.start()
         else:
-            post_send[step] = block.astype(BF)
             copy = pltpu.make_async_remote_copy(
-                src_ref=post_send.at[step], dst_ref=post_recv.at[step],
+                src_ref=post_send.at[step], dst_ref=post_recv.at[me],
                 send_sem=post_ssem.at[step], recv_sem=post_rsem.at[step],
                 device_id={"blk": other // n_dp, "dp": lax.rem(other, n_dp)},
                 device_id_type=MESH,
@@ -265,12 +242,62 @@
             copy.start()
             post_copies.append(copy)
 
-    total = kept[blk]
+    for block in range(half // COLS):
+        source = pl.ds(pl.multiple_of(core * half + block * COLS, COLS), COLS)
+        local = pl.ds(block * COLS, COLS)
+        kept[:, :, local] = dot_nn(low[...], mod[:, source]).reshape(n_blk, PAD, COLS)
+    class_send[...] = dot_nt(
+        weights[...], onehot_t[...], precision=lax.Precision.HIGHEST
+    ).reshape(n_blk, PAD, LANES)
+    chip_copies = []
+    for step in range(1, n_blk):
+        target = lax.rem(blk + step, n_blk)
+        copy = pltpu.make_async_remote_copy(
+            src_ref=class_send.at[target], dst_ref=class_recv.at[step],
+            send_sem=class_ssem.at[step], recv_sem=class_rsem.at[step],
+            device_id={"blk": target}, device_id_type=MESH,
+        )
+        copy.start()
+        chip_copies.append(copy)
+    side_copies = []
+    for block, copy in enumerate(mate_copies):
+        copy.wait_recv()
+        local = pl.ds(block * COLS, COLS)
+        both = kept[:, :, local] + mate_recv[:, :, local].astype(F32)
+        both = both.reshape(deep, near, PAD, COLS)
+        kept[0:deep, :, local] = jnp.where(y == 0, both[:, 0], both[:, 1])
+        side_send[:, :, local] = jnp.where(y == 0, both[:, 1], both[:, 0]).astype(BF)
+        copy = pltpu.make_async_remote_copy(
+            src_ref=side_send.at[:, :, local], dst_ref=side_recv.at[:, :, local],
+            send_sem=side_ssem.at[block], recv_sem=side_rsem.at[block],
+            device_id=partner, device_id_type=MESH,
+        )
+        copy.start()
+        side_copies.append(copy)
+    for block, copy in enumerate(side_copies):
+        copy.wait_recv()
+        local = pl.ds(block * COLS, COLS)
+        both = kept[0:deep, :, local] + side_recv[:, :, local].astype(F32)
+        kept[0:deep, :, local] = both
+        chip_send[:, :, local] = both.astype(BF)
+        for step in range(1, deep):
+            target = lax.rem(z + step, deep)
+            copy = pltpu.make_async_remote_copy(
+                src_ref=chip_send.at[target, :, local],
+                dst_ref=chip_recv.at[step, :, local],
+                send_sem=chip_ssem.at[step, block], recv_sem=chip_rsem.at[step, block],
+                device_id={"blk": target * near + y}, device_id_type=MESH,
+            )
+            copy.start()
+            chip_copies.append(copy)
+
+    total = kept[z]
     classes = class_send[blk]
     for copy in chip_copies:
         copy.wait_recv()
+    for step in range(1, deep):
+        total = total + chip_recv[step].astype(F32)
     for step in range(1, n_blk):
-        total = total + chip_recv[step].astype(F32)
         classes = classes + class_recv[step]
     first, second = total[0:rows_mine], total[rows_mine:own_rows]
     final_send[0:rows_mine, :] = jnp.where(core == 0, second, first)
@@ -286,26 +313,31 @@
         finals.append(copy)
     sums_out[:, my_cols] = jnp.where(core == 0, first, second)
 
-    for step in [0] + list(range(1, devices)):
-        if step:
-            post_copies[step - 1].wait_recv()
-    for source in range(devices):
-        step = lax.rem(me + devices - source, devices)
-        post_out[:, source * capacity:(source + 1) * capacity] = post_recv[step].astype(F32)
-
     for copy in finals:
         copy.wait_recv()
     sums_out[:, mate_cols] = final_recv[0:rows_mine, :]
     classes = classes + cfinal_recv[...]
     mine = jnp.where(core == 0, classes[0:rows_mine], classes[rows_mine:own_rows])
-    mine = mine[:, 0:kinds]
-
+    class_out[0:rows_mine, :] = mine
+    for copy in post_copies:
+        copy.wait_recv()
+    own_copy.wait()
+
+    for copy in far_copies[1:] + near_copies + forwards + mate_copies + side_copies + chip_copies + post_copies + finals:
+        copy.wait_send()
+
+
+def finish(sums_in, class_in, ctf_in, post_in, sums_out, ctf_out, post_out):
+    kinds = ctf_in.shape[0]
+    rows_mine = sums_in.shape[0]
+    capacity = post_in.shape[2]
+    for source in range(post_in.shape[0]):
+        post_out[:, source * capacity:(source + 1) * capacity] = post_in[source].astype(F32)
+    sums_out[...] = sums_in[...]
+    ctf = ctf_in[...]
     ctf_out[...] = dot_nn(
-        mine, ctf_in[...] * ctf_in[...], precision=lax.Precision.HIGHEST
-    )
-
-    for copy in ref_copies + forwards + mate_copies + chip_copies + post_copies + finals:
-        copy.wait_send()
+        class_in[0:rows_mine, 0:kinds], ctf * ctf, precision=lax.Precision.HIGHEST
+    )
 
 
 def per_device(particles, defocus, pick_dest, references, ctf_table):
@@ -320,15 +352,15 @@
     rows_mine = own_rows // n_dp
     vmem = pl.BlockSpec(memory_space=pltpu.VMEM)
     dma = pltpu.SemaphoreType.DMA
-    sums, weights, posterior = pl.pallas_call(
+    sums, classes, posterior = pl.pallas_call(
         functools.partial(kernel, n_blk, n_dp, own_rows, capacity),
         out_shape=(
             jax.ShapeDtypeStruct((rows_mine, pix), F32),
-            jax.ShapeDtypeStruct((rows_mine, pix), F32),
-            jax.ShapeDtypeStruct((kept_refs, devices * capacity), F32),
+            jax.ShapeDtypeStruct((8, LANES), F32),
+            jax.ShapeDtypeStruct((devices, kept_refs, capacity), BF),
         ),
         in_specs=[pl.BlockSpec(memory_space=pl.ANY), vmem, vmem, vmem, vmem],
-        out_specs=(vmem, vmem, vmem),
+        out_specs=(vmem, vmem, pl.BlockSpec(memory_space=pl.ANY)),
         scratch_shapes=[
             pltpu.VMEM((held, pix), BF),
             pltpu.VMEM((n_blk, PAD, pix), BF),
@@ -342,8 +374,10 @@
             pltpu.VMEM((n_blk, PAD, half), F32),
             pltpu.VMEM((n_blk, PAD, half), BF),
             pltpu.VMEM((n_blk, PAD, half), BF),
-            pltpu.VMEM((n_blk, PAD, half), BF),
-            pltpu.VMEM((n_blk, PAD, half), BF),
+            pltpu.VMEM((n_blk // 2, PAD, half), BF),
+            pltpu.VMEM((n_blk // 2, PAD, half), BF),
+            pltpu.VMEM((n_blk // 2, PAD, half), BF),
+            pltpu.VMEM((n_blk // 2, PAD, half), BF),
             pltpu.VMEM((n_blk, PAD, LANES), F32),
             pltpu.VMEM((n_blk, PAD, LANES), F32),
             pltpu.VMEM((8, half), F32),
@@ -351,12 +385,14 @@
             pltpu.VMEM((PAD, LANES), F32),
             pltpu.VMEM((PAD, LANES), F32),
             pltpu.VMEM((devices, kept_refs, capacity), BF),
-            pltpu.VMEM((devices, kept_refs, capacity), BF),
             dma((held // ROWS,)),
             dma((n_blk,)), dma((n_blk,)), dma((n_blk,)), dma((n_blk,)),
+            dma((n_blk,)), dma((n_blk,)),
             dma((devices,)), dma((devices,)),
             dma((half // COLS,)), dma((half // COLS,)),
-            dma((n_blk,)), dma((n_blk,)), dma((n_blk,)), dma((n_blk,)),
+            dma((half // COLS,)), dma((half // COLS,)),
+            dma((n_blk // 2, half // COLS)), dma((n_blk // 2, half // COLS)),
+            dma((n_blk,)), dma((n_blk,)),
             dma((2,)), dma((2,)),
         ],
         compiler_params=pltpu.CompilerParams(
@@ -370,6 +406,18 @@
         references,
         ctf_table,
     )
+    sums, weights, posterior = pl.pallas_call(
+        finish,
+        out_shape=(
+            jax.ShapeDtypeStruct((rows_mine, pix), F32),
+            jax.ShapeDtypeStruct((rows_mine, pix), F32),
+            jax.ShapeDtypeStruct((kept_refs, devices * capacity), F32),
+        ),
+        in_specs=[vmem, vmem, vmem, vmem],
+        out_specs=(vmem, vmem, vmem),
+        compiler_params=pltpu.CompilerParams(vmem_limit_bytes=40 << 20),
+        name="em_finish",
+    )(sums, classes, ctf_table, posterior)
     return sums, weights, posterior.T
 
 

time: 58.6 us -> 49.2 us (0.84)
  the two profiles are of different devices: /device:TPU:13 before, /device:TPU:0 now
where the time goes in v2:
time: 49.2 us; the launch traced here: 49 us
  Pallas kernels  45.7 us (93%)
  local copies, waits for them, and re-layouts  2.56 us (5%)
  between operations  0.67 us (1%)
    pallas_call x1, Pallas kernels, per_device(): pl.pallas_call(functools.partial(kernel, n_blk, n_dp, own_rows, capacity)...  44.5 us
    unnamed x8, local copies, waits for them, and re-layouts  2.56 us
    pallas_call x1, Pallas kernels, per_device(): pl.pallas_call(finish, out_shape=(jax.ShapeDtypeStruct((rows_mine, pix),...  1.26 us

profile of v2, /device:TPU:0, one launch (start us, length us, event | category | flops | bytes accessed | tf_op | source)
XLA Modules:
  0.0 49.0 jit_solution(14040952811336479202)
XLA Ops:
  0.6 0.0 copy-start
  0.6 44.5 %em_step.1 = (f32[6,4096]{1,0:T(8,128)}, f32[8,128]{1,0:T(8,128)}, bf16[16,96,128]{2,1,0:T(8,128)(2,1)}) custom-call(bf16[1024,4096]{1,0:T(8,128)(2,1)} %particles.1, s32[1,1024]{1,0:T(1,128)} %bitcast.3, s32[1,1024]{1,0:T(1,128)} %bitcast.4, bf16[12,4096]{1,0:T(8,128)(2,1)} %refs_in.1, f32[16,4096]{1,0:T(8,128)} %ctf_in.3), custom_call_target="tpu_custom_call" | custom-call | tf_op jit(solution)/shard_map/em_step/pallas_call | solution.py:355
  45.1 0.0 copy-done
  45.1 0.0 copy-start.1
  45.1 1.0 %copy-done.1 = bf16[16,96,128]{2,1,0:T(8,128)(2,1)S(1)} copy-done((bf16[16,96,128]{2,1,0:T(8,128)(2,1)S(1)}, bf16[16,96,128]{2,1,0:T(8,128)(2,1)}, u32[]{:S(2)}) %copy-start.1) | copy-done | bytes 393240
  46.1 0.0 copy-start.2
  46.1 0.9 %copy-done.2 = f32[6,4096]{1,0:T(8,128)S(1)} copy-done((f32[6,4096]{1,0:T(8,128)S(1)}, f32[6,4096]{1,0:T(8,128)}, u32[]{:S(2)}) %copy-start.2) | copy-done | bytes 98328
  47.0 0.0 copy-start.3
  47.0 0.7 %copy-done.3 = f32[8,128]{1,0:T(8,128)S(1)} copy-done((f32[8,128]{1,0:T(8,128)S(1)}, f32[8,128]{1,0:T(8,128)}, u32[]{:S(2)}) %copy-start.3) | copy-done | bytes 4120
  47.7 1.3 %em_finish.1 = (f32[6,4096]{1,0:T(8,128)}, f32[6,4096]{1,0:T(8,128)}, f32[96,2048]{1,0:T(8,128)}) custom-call(f32[6,4096]{1,0:T(8,128)S(1)} %copy-done.2, f32[8,128]{1,0:T(8,128)S(1)} %copy-done.3, f32[16,4096]{1,0:T(8,128)S(1)} %copy-done, bf16[16,96,128]{2,1,0:T(8,128)(2,1)S(1)} %copy-done.1), custom_call_target="tpu_custom_call" | custom-call | tf_op jit(solution)/shard_map/em_finish/pallas_call | solution.py:409
Async XLA Ops:
  0.6 44.5 %copy-start = (f32[16,4096]{1,0:T(8,128)S(1)}, f32[16,4096]{1,0:T(8,128)}, u32[]{:S(2)}) copy-start(f32[16,4096]{1,0:T(8,128)} %ctf_in.3) | copy-start | bytes 786436
  45.1 1.0 %copy-start.1 = (bf16[16,96,128]{2,1,0:T(8,128)(2,1)S(1)}, bf16[16,96,128]{2,1,0:T(8,128)(2,1)}, u32[]{:S(2)}) copy-start(bf16[16,96,128]{2,1,0:T(8,128)(2,1)} %get-tuple-element.11.post_in) | copy-start | bytes 1179652
  46.1 0.9 %copy-start.2 = (f32[6,4096]{1,0:T(8,128)S(1)}, f32[6,4096]{1,0:T(8,128)}, u32[]{:S(2)}) copy-start(f32[6,4096]{1,0:T(8,128)} %get-tuple-element.9.sums_in) | copy-start | bytes 294916
  47.0 0.7 %copy-start.3 = (f32[8,128]{1,0:T(8,128)S(1)}, f32[8,128]{1,0:T(8,128)}, u32[]{:S(2)}) copy-start(f32[8,128]{1,0:T(8,128)} %get-tuple-element.10.class_in) | copy-start | bytes 12292
